TPU v7x, 256 devices: a whole 4x4x8 slice. The times are simulated.
256 devices in a mesh: group: 8 (over z_lo, y), dev: 32 (over x, z_hi, core).
Axes of the slice: x: 4, y: 4, z: 8 (z_hi: 4, z_lo: 2; z = z_hi * 2 + z_lo), core: 2. Of those that a mesh axis runs over, the one named last changes fastest.
Arguments:
- hidden_rows: bfloat16 [8192, 8192], P(('group', 'dev')), may hold values from -6 to 6
- norm_gain: float32 [8192], replicated, may hold values from 0.1 to 1.9
- query_weight: bfloat16 [8192, 8192], P('group', 'dev'), may hold values from -0.0625 to 0.0625
- key_weight: bfloat16 [8192, 1024], P('group'), may hold values from -0.0625 to 0.0625
- value_weight: bfloat16 [8192, 1024], P('group'), may hold values from -0.0625 to 0.0625
- packing: int32 [8, 1024], P('group'), may hold values from 0 to 1023, each once within a row
- segment_ids: int32 [8, 1024], P('group'), may hold values from 0 to 15, never falling along the last dimension, each value on 1 to 256 neighbouring positions
Outputs:
- context: bfloat16 [8192, 8192], P('group', 'dev')
Inputs may be any that keep to these rules, and one draw needn't show every extreme that they name: Each row of packing holds every number below 1024 once. `segment_ids`: along each row segment numbers never fall; each response has 1 to 256 slots and one has exactly 256.
All inputs are finite; a program needn't handle non-finite values.
Results may differ from a plain program's by a relative error of at most 0.0076.
Values may be sent and summed in bfloat16 or wider, within the bound.
A program may use at most 128 MiB of HBM per device.

v0:
```python
import math

import jax
import jax.numpy as jnp
from jax import lax
from jax.sharding import PartitionSpec as P

HEADS = 64
KV = 8
HDIM = 128


def normalize(rows, gain):
    widened = rows.astype(jnp.float32)
    inverse = lax.rsqrt(jnp.mean(widened * widened, axis=1, keepdims=True) + 1e-06)
    return (widened * inverse * gain).astype(jnp.bfloat16)


def per_device(
    hidden_rows, norm_gain, query_weight, key_weight, value_weight, packing, segment_ids
):
    heads_here = query_weight.shape[1] // HDIM
    dev_index = lax.axis_index("dev")
    kv_head = dev_index * heads_here // (HEADS // KV)
    key_columns = lax.dynamic_slice_in_dim(key_weight, kv_head * HDIM, HDIM, 1)
    value_columns = lax.dynamic_slice_in_dim(value_weight, kv_head * HDIM, HDIM, 1)
    source = normalize(hidden_rows, norm_gain)
    gathered = lax.all_gather(source, "dev", axis=0, tiled=True)

    def add_rows(weight_rows):
        return jnp.dot(gathered, weight_rows, preferred_element_type=jnp.float32)

    query_out = add_rows(lax.all_gather(query_weight, "group", axis=0, tiled=True))
    weight_rows = (
        lax.all_gather(key_columns, "group", axis=0, tiled=True),
        lax.all_gather(value_columns, "group", axis=0, tiled=True),
    )
    key_out = add_rows(weight_rows[0])
    value_out = add_rows(weight_rows[1])
    query = query_out.astype(jnp.bfloat16)
    key_rows = key_out.astype(jnp.bfloat16)
    value_rows = value_out.astype(jnp.bfloat16)
    order = packing[0]
    query = query[order]
    key_rows = key_rows[order]
    value_rows = value_rows[order]
    slots = query.shape[0]
    query_heads = query.reshape(slots, heads_here, HDIM)
    segment = segment_ids[0]
    position = jnp.arange(slots, dtype=jnp.int32)
    allowed = (segment[:, None] == segment[None, :]) & (position[None, :] <= position[:, None])
    scores = jnp.einsum(
        "ihd,jd->hij", query_heads, key_rows, preferred_element_type=jnp.float32
    ) / math.sqrt(HDIM)
    powers = jnp.where(allowed[None], jnp.exp(scores), 0.0)
    attend = (powers / jnp.sum(powers, axis=2, keepdims=True)).astype(jnp.bfloat16)
    mixed = jnp.einsum("hij,jd->ihd", attend, value_rows, preferred_element_type=jnp.float32)
    return mixed.astype(jnp.bfloat16).reshape(slots, heads_here * HDIM)


def solution(mesh):
    in_specs = (
        P(("group", "dev"), None),
        P(),
        P("group", "dev"),
        P("group", None),
        P("group", None),
        P("group", None),
        P("group", None),
    )
    out_specs = P("group", "dev")
    return jax.shard_map(
        per_device, mesh=mesh, in_specs=in_specs, out_specs=out_specs, check_vma=False
    )
```

profile of v0, /device:TPU:1, one launch (start us, length us, event | category | flops | bytes accessed | tf_op | source)
XLA Modules:
  0.0 307.1 jit_solution(6572861401144411389)
XLA Ops:
  6.5 0.0 copy-start
  6.5 0.0 all-gather.7.cloned.1.call-start
  6.5 1.6 copy-done
  8.1 0.8 constant_dynamic-slice_fusion.1
  8.9 0.0 all-gather.7.cloned.1.call-update
  8.9 0.0 all-gather.5.cloned.1.call-start
  9.0 1.3 fusion.4
  10.2 2.0 fusion.6
  12.3 0.0 all-gather.5.cloned.1.call-update
  12.3 0.0 all-gather.9.cloned.1.call-start
  12.3 1.7 constant_dynamic-slice_fusion
  14.0 0.0 all-gather.9.cloned.1.call-update
  14.0 0.0 all-gather.11.cloned.1.call-start
  14.1 0.5 all-gather.11.cloned.1.call-update
  14.6 0.7 compare_select_fusion
  15.3 2.4 fusion.1
  17.7 34.5 %all-gather.7.cloned.1.call-done = bf16[8192,128]{1,0:T(8,128)(2,1)} async-done(((bf16[1024,128]{1,0:T(8,128)(2,1)}), bf16[8192,128]{1,0:T(8,128)(2,1)}) %all-gather.7.cloned.1.call-update) | async-done | bytes 2097168 | tf_op jit(solution)/shard_map/all_gather | solution.py:36
  52.3 112.2 %all-gather.5.cloned.1.call-done = bf16[1024,8192]{1,0:T(8,128)(2,1)} async-done(((bf16[32,8192]{1,0:T(8,128)(2,1)}), bf16[1024,8192]{1,0:T(8,128)(2,1)}) %all-gather.5.cloned.1.call-update) | async-done | bytes 16777232 | tf_op jit(solution)/shard_map/all_gather | solution.py:28
  164.5 10.8 %convolution_convert_fusion.2 = bf16[1024,128]{1,0:T(8,128)(2,1)S(1)} fusion(bf16[1024,8192]{1,0:T(8,128)(2,1)} %all-gather.5.cloned.1.call-done, bf16[8192,128]{1,0:T(8,128)(2,1)} %all-gather.7.cloned.1.call-done), kind=kOutput, calls=%fused_computation.14 | convolution fusion | flops 2147614720 | bytes 19136512 | tf_op jit(solution)/shard_map/dot_general | solution.py:31
  175.3 3.4 %gather_fusion = bf16[1024,128]{1,0:T(8,128)(2,1)S(1)} fusion(bf16[1024,128]{1,0:T(8,128)(2,1)S(1)} %convolution_convert_fusion.2, s32[1024]{0:T(1024)S(1)} %broadcast_clamp_fusion), kind=kCustom, calls=%fused_computation | custom fusion | bytes 528384 | tf_op jit(solution)/shard_map/gather | solution.py:46
  178.7 37.9 %all-gather.9.cloned.1.call-done = bf16[8192,128]{1,0:T(8,128)(2,1)} async-done(((bf16[1024,128]{1,0:T(8,128)(2,1)}), bf16[8192,128]{1,0:T(8,128)(2,1)}) %all-gather.9.cloned.1.call-update) | async-done | bytes 2097168 | tf_op jit(solution)/shard_map/all_gather | solution.py:35
  216.6 10.8 %convolution_convert_fusion.1 = bf16[1024,128]{1,0:T(8,128)(2,1)S(1)} fusion(bf16[1024,8192]{1,0:T(8,128)(2,1)} %all-gather.5.cloned.1.call-done, bf16[8192,128]{1,0:T(8,128)(2,1)} %all-gather.9.cloned.1.call-done), kind=kOutput, calls=%fused_computation.13 | convolution fusion | flops 2147614720 | bytes 19136512 | tf_op jit(solution)/shard_map/dot_general | solution.py:31
  227.5 4.3 %gather_fusion.1 = bf16[1024,128]{1,0:T(8,128)(2,1)} fusion(bf16[1024,128]{1,0:T(8,128)(2,1)S(1)} %convolution_convert_fusion.1, s32[1024]{0:T(1024)S(1)} %broadcast_clamp_fusion), kind=kCustom, calls=%fused_computation.1 | custom fusion | bytes 528384 | tf_op jit(solution)/shard_map/gather | solution.py:45
  231.8 45.8 %all-gather.11.cloned.1.call-done = bf16[8192,256]{1,0:T(8,128)(2,1)} async-done(((bf16[1024,256]{1,0:T(8,128)(2,1)}), bf16[8192,256]{1,0:T(8,128)(2,1)}) %all-gather.11.cloned.1.call-update) | async-done | bytes 4194320 | tf_op jit(solution)/shard_map/all_gather | solution.py:33
  277.6 11.4 %convolution_convert_fusion = bf16[1024,256]{1,0:T(8,128)(2,1)S(1)} fusion(bf16[1024,8192]{1,0:T(8,128)(2,1)} %all-gather.5.cloned.1.call-done, bf16[8192,256]{1,0:T(8,128)(2,1)} %all-gather.11.cloned.1.call-done), kind=kOutput, calls=%fused_computation.12 | convolution fusion | flops 4295229440 | bytes 21495808 | tf_op jit(solution)/shard_map/dot_general | solution.py:31
  289.1 3.9 %gather_fusion.2 = bf16[1024,256]{1,0:T(8,128)(2,1)S(1)} fusion(bf16[1024,256]{1,0:T(8,128)(2,1)S(1)} %convolution_convert_fusion, s32[1024]{0:T(1024)S(1)} %broadcast_clamp_fusion), kind=kCustom, calls=%fused_computation.2 | custom fusion | bytes 1052672 | tf_op jit(solution)/shard_map/gather | solution.py:44
  293.0 0.0 copy-start.1
  293.0 3.7 %fusion = (f32[2,1024]{1,0:T(2,128)S(1)}, f32[1024,1024,2]{1,0,2:T(8,128)S(1)}) fusion(pred[1024,1024]{0,1:T(8,128)(4,1)} %fusion.1, bf16[1024,128]{1,0:T(8,128)(2,1)} %gather_fusion.1, bf16[1024,256]{1,0:T(8,128)(2,1)S(1)} %gather_fusion.2), kind=kOutput, calls=%fused_computation.5 | convolution fusion | flops 543160320 | bytes 10231808 | tf_op jit(solution)/shard_map/ihd,jd->hij/dot_general | solution.py:52
  296.7 0.0 copy-done.1
  296.8 2.8 fusion.3
  299.6 1.0 copy.15
  (2 shorter events, 0.0 us)
Async XLA Ops:
  6.5 1.6 copy-start
  6.5 45.7 %all-gather.7.cloned.1.call-start = ((), (), s32[]{:S(2)}) async-start(), calls=%async_computation.1 | async-start | bytes 2359296 | tf_op jit(solution)/shard_map/all_gather | solution.py:36
  8.9 155.6 %all-gather.5.cloned.1.call-start = ((), (), s32[]{:S(2)}) async-start(), calls=%async_computation | async-start | bytes 17301504 | tf_op jit(solution)/shard_map/all_gather | solution.py:28
  12.3 204.4 %all-gather.9.cloned.1.call-start = ((), (), s32[]{:S(2)}) async-start(), calls=%async_computation.2 | async-start | bytes 2359296 | tf_op jit(solution)/shard_map/all_gather | solution.py:35
  14.0 263.6 %all-gather.11.cloned.1.call-start = ((), (), s32[]{:S(2)}) async-start(), calls=%async_computation.3 | async-start | bytes 4718592 | tf_op jit(solution)/shard_map/all_gather | solution.py:33
  293.0 3.7 %copy-start.1 = (pred[1024,1024]{0,1:T(8,128)(4,1)S(1)}, pred[1024,1024]{0,1:T(8,128)(4,1)}, u32[]{:S(2)}) copy-start(pred[1024,1024]{0,1:T(8,128)(4,1)} %fusion.1) | copy-start | bytes 3145732
Sparse Core Ops, SparseCore 0:
  9.1 43.0 all-gather.6
  54.8 109.6 all-gather.4
  166.3 50.3 all-gather.8
  218.3 59.2 all-gather.10
where the time goes:
time: 307 us
  waiting for transfers between devices  231 us (75%)
  matrix products  39.6 us (13%)
  local copies, waits for them, and re-layouts  16.7 us (5%)
  between operations  13.2 us (4%)
  other arithmetic  6.41 us (2%)
    all_gather x1, waiting for transfers between devices, per_device(): gathered = lax.all_gather(source, 'dev', axis=0, tiled=True)  112 us
    all_gather x1, waiting for transfers between devices, per_device(): lax.all_gather(query_weight, 'group', axis=0, tiled=True)  45.8 us
    all_gather x1, waiting for transfers between devices, per_device(): lax.all_gather(key_columns, 'group', axis=0, tiled=True)  37.9 us
    all_gather x1, waiting for transfers between devices, per_device(): lax.all_gather(value_columns, 'group', axis=0, tiled=True)  34.5 us
    dot_general x3, matrix products, add_rows(): return jnp.dot(gathered, weight_rows, preferred_element_type=jnp.float32)  33.1 us
  transfers between devices with their start and end apart: 4, of which 4 were waited for; matrix products, arithmetic and copies ran while one was open for 12% of the time, Pallas kernels for 0%

commit v1 on v0

v1 whole, which is shorter than its diff:
```python
import math

import jax
import jax.numpy as jnp
from jax import lax
from jax.experimental import pallas as pl
from jax.experimental.pallas import tpu as pltpu
from jax.sharding import PartitionSpec as P

HDIM = 128
MESH = pl.DeviceIdType.MESH
EPS = 1e-06
COPIES = 92
SHIFT = (0, 3, 1, 2)


def project_kernel(
    x_ref, gain_ref, wq_ref, wk_ref, wv_ref, out_ref, xbuf, wbuf, acc, send_sem, recv_sem, local_sem
):
    g = lax.axis_index("group")
    d = lax.axis_index("dev")
    zl, y = g // 4, g % 4
    x, zh, c = d // 8, (d // 2) % 4, d % 2
    rows = x_ref.shape[0]
    half = rows // 2
    slab = wq_ref.shape[0]
    wide = wq_ref.shape[1]

    def dev_at(dx, dz, core):
        return (((x + dx) % 4) * 4 + (zh + dz) % 4) * 2 + core

    right, left = (g, dev_at(1, 0, c)), (g, dev_at(3, 0, c))
    up, down = (g, dev_at(0, 1, c)), (g, dev_at(0, 3, c))
    sibling = (g, dev_at(0, 0, 1 - c))
    across = ((1 - zl) * 4 + y, d)
    north, south = (zl * 4 + (y + 1) % 4, d), (zl * 4 + (y + 3) % 4, d)

    barrier = pltpu.get_barrier_semaphore()
    partners = (right, left, up, down, sibling, across, north, south)
    for partner in partners:
        pl.semaphore_signal(barrier, inc=1, device_id=partner, device_id_type=MESH)

    def xslot(zr, xr, cr, h):
        return xbuf.at[pl.ds((((zr * 4 + xr) * 2 + cr) * 2 + h) * half, half), :]

    def slab_at(zlr, yr):
        zl_of = zl if zlr == 0 else 1 - zl
        return (zl_of * 4 + (y + SHIFT[yr]) % 4) * slab

    def wslot(zlr, yr, h):
        start = pl.multiple_of(slab_at(zlr, yr) + h * (slab // 2), slab // 2)
        return wbuf.at[pl.ds(start, slab // 2), pl.ds(0, wide + HDIM)]

    def kvslot(zlr, yr, h, which):
        start = pl.multiple_of(slab_at(zlr, yr) + h * (slab // 2), slab // 2)
        return wbuf.at[pl.ds(start, slab // 2), pl.ds(wide + which * HDIM, HDIM)]

    index = {}
    started = []

    def number(key):
        return index.setdefault(key, len(index))

    def describe(key, src, dst, device):
        i = number(key)
        return pltpu.make_async_remote_copy(
            src_ref=src,
            dst_ref=dst,
            send_sem=send_sem.at[i],
            recv_sem=recv_sem.at[i],
            device_id=device,
            device_id_type=MESH,
        )

    def send(key, src, dst, device):
        copy = describe(key, src, dst, device)
        copy.start()
        started.append(copy)

    def arrive(key, dst):
        describe(key, dst, dst, sibling).wait_recv()

    def share_x(zr, xr, h):
        send(("s", zr, xr, h), xslot(zr, xr, 0, h), xslot(zr, xr, 1, h), sibling)

    def share_kv(zlr, yr, h):
        send(("k", zlr, yr, h), kvslot(zlr, yr, h, 0), kvslot(zlr, yr, h, 1), sibling)

    def spread_x(zr, h):
        send(("r", zr, h), xslot(zr, 0, 0, h), xslot(zr, 1, 0, h), right)
        send(("l", zr, h), xslot(zr, 0, 0, h), xslot(zr, 2, 0, h), left)

    def from_left(zr, h):
        arrive(("r", zr, h), xslot(zr, 1, 0, h))
        if h == 0:
            send(("ro", zr), xslot(zr, 1, 0, 0), xslot(zr, 3, 0, 0), right)
        share_x(zr, 1, h)

    def from_right(zr, h):
        arrive(("l", zr, h), xslot(zr, 2, 0, h))
        if h == 1:
            send(("lo", zr), xslot(zr, 2, 0, 1), xslot(zr, 3, 0, 1), left)
        share_x(zr, 2, h)

    def from_opposite(zr):
        arrive(("ro", zr), xslot(zr, 3, 0, 0))
        share_x(zr, 3, 0)
        arrive(("lo", zr), xslot(zr, 3, 0, 1))
        share_x(zr, 3, 1)

    def spread_w(zlr, h):
        send(("n", zlr, h), wslot(zlr, 0, h), wslot(zlr, 0, h), north)
        send(("t", zlr, h), wslot(zlr, 0, h), wslot(zlr, 0, h), south)

    def from_south(zlr, h):
        arrive(("n", zlr, h), wslot(zlr, 1, h))
        if h == 0:
            send(("no", zlr), wslot(zlr, 1, 0), wslot(zlr, 1, 0), north)
        share_kv(zlr, 1, h)

    def from_north(zlr, h):
        arrive(("t", zlr, h), wslot(zlr, 2, h))
        if h == 1:
            send(("to", zlr), wslot(zlr, 2, 1), wslot(zlr, 2, 1), south)
        share_kv(zlr, 2, h)

    def from_far(zlr):
        arrive(("no", zlr), wslot(zlr, 3, 0))
        share_kv(zlr, 3, 0)
        arrive(("to", zlr), wslot(zlr, 3, 1))
        share_kv(zlr, 3, 1)

    def from_below(h):
        arrive(("u", h), xslot(1, 0, 0, h))
        if h == 0:
            send(("uo",), xslot(1, 0, 0, 0), xslot(3, 0, 0, 0), up)
        spread_x(1, h)
        share_x(1, 0, h)

    def from_above(h):
        arrive(("d", h), xslot(2, 0, 0, h))
        if h == 1:
            send(("do",), xslot(2, 0, 0, 1), xslot(3, 0, 0, 1), down)
        spread_x(2, h)
        share_x(2, 0, h)

    def from_across(h):
        arrive(("a", h), wslot(1, 0, h))
        spread_w(1, h)
        share_kv(1, 0, h)

    own = pl.multiple_of(slab_at(0, 0), slab)
    own_q = pltpu.make_async_copy(
        wq_ref, wbuf.at[pl.ds(own, slab), pl.ds(0, wide)], local_sem.at[0]
    )
    own_q.start()
    column = pl.multiple_of((d * (wide // HDIM) // 8) * HDIM, HDIM)

    def own_kv(source):
        return pltpu.make_async_copy(
            source.at[:, pl.ds(column, HDIM)],
            wbuf.at[pl.ds(own, slab), pl.ds(wide, HDIM)],
            local_sem.at[1],
        )

    @pl.when(c == 0)
    def _():
        own_kv(wk_ref).start()

    @pl.when(c == 1)
    def _():
        own_kv(wv_ref).start()

    widened = x_ref[...].astype(jnp.float32)
    inverse = lax.rsqrt(jnp.mean(widened * widened, axis=1, keepdims=True) + EPS)
    xbuf[pl.ds(0, half), :] = (widened[:half] * inverse[:half] * gain_ref[...]).astype(jnp.bfloat16)
    xbuf[pl.ds(half, half), :] = (widened[half:] * inverse[half:] * gain_ref[...]).astype(jnp.bfloat16)

    own_q.wait()
    own_kv(wk_ref).wait()
    pl.semaphore_wait(barrier, len(partners))

    send(("r", 0, 0), xslot(0, 0, 0, 0), xslot(0, 1, 0, 0), right)
    send(("l", 0, 1), xslot(0, 0, 0, 1), xslot(0, 2, 0, 1), left)
    send(("u", 0), xslot(0, 0, 0, 0), xslot(1, 0, 0, 0), up)
    send(("d", 1), xslot(0, 0, 0, 1), xslot(2, 0, 0, 1), down)
    send(("n", 0, 0), wslot(0, 0, 0), wslot(0, 0, 0), north)
    send(("t", 0, 1), wslot(0, 0, 1), wslot(0, 0, 1), south)
    send(("a", 0), wslot(0, 0, 0), wslot(0, 0, 0), across)
    send(("r", 0, 1), xslot(0, 0, 0, 1), xslot(0, 1, 0, 1), right)
    send(("l", 0, 0), xslot(0, 0, 0, 0), xslot(0, 2, 0, 0), left)
    send(("u", 1), xslot(0, 0, 0, 1), xslot(1, 0, 0, 1), up)
    send(("d", 0), xslot(0, 0, 0, 0), xslot(2, 0, 0, 0), down)
    send(("n", 0, 1), wslot(0, 0, 1), wslot(0, 0, 1), north)
    send(("t", 0, 0), wslot(0, 0, 0), wslot(0, 0, 0), south)
    send(("a", 1), wslot(0, 0, 1), wslot(0, 0, 1), across)
    for h in (0, 1):
        share_x(0, 0, h)
        share_kv(0, 0, h)

    from_left(0, 0)
    from_right(0, 1)
    from_south(0, 0)
    from_north(0, 1)
    from_left(0, 1)
    from_right(0, 0)
    from_below(0)
    from_above(1)
    from_south(0, 1)
    from_north(0, 0)
    from_opposite(0)
    from_across(0)
    from_below(1)
    from_above(0)
    from_left(1, 0)
    from_right(2, 1)
    from_across(1)
    from_far(0)
    from_right(1, 0)
    from_left(2, 1)
    arrive(("uo",), xslot(3, 0, 0, 0))
    spread_x(3, 0)
    share_x(3, 0, 0)
    arrive(("do",), xslot(3, 0, 0, 1))
    spread_x(3, 1)
    share_x(3, 0, 1)
    from_right(1, 1)
    from_left(2, 0)
    from_south(1, 0)
    from_north(1, 1)
    from_left(1, 1)
    from_right(2, 0)
    from_south(1, 1)
    from_north(1, 0)
    from_opposite(1)
    from_opposite(2)
    from_far(1)

    def shared_x(zr):
        for xr in range(4):
            for h in (0, 1):
                arrive(("s", zr, xr, h), xslot(zr, xr, 1, h))

    def project(zr):
        count = 8 * rows
        acc[...] = jnp.zeros_like(acc)

        def step(k, carry):
            at = pl.ds(pl.multiple_of(k * slab, slab), slab)
            acc[...] += jnp.dot(
                xbuf[pl.ds(zr * count, count), at], wbuf[at, :], preferred_element_type=jnp.float32
            )
            return carry

        lax.fori_loop(0, 8, step, 0)
        for xr in range(4):
            for cr in range(2):
                core = c if cr == 0 else 1 - c
                to = pl.multiple_of(dev_at(SHIFT[xr], SHIFT[zr], core) * rows, rows)
                out_ref[pl.ds(to, rows), :] = acc[pl.ds((xr * 2 + cr) * rows, rows), :].astype(
                    jnp.bfloat16
                )

    for zlr in range(2):
        for yr in range(4):
            for h in (0, 1):
                arrive(("k", zlr, yr, h), kvslot(zlr, yr, h, 1))
    shared_x(0)
    project(0)
    from_left(3, 0)
    from_right(3, 1)
    shared_x(1)
    project(1)
    from_left(3, 1)
    from_right(3, 0)
    shared_x(2)
    project(2)
    from_opposite(3)
    shared_x(3)
    project(3)
    for copy in started:
        copy.wait_send()


def project_rows(rows, gain, query_weight, key_weight, value_weight):
    tokens, width = rows.shape
    slab, wide = query_weight.shape
    packed = wide + 2 * HDIM
    return pl.pallas_call(
        project_kernel,
        out_shape=jax.ShapeDtypeStruct((32 * tokens, packed), jnp.bfloat16),
        in_specs=[
            pl.BlockSpec(memory_space=pltpu.VMEM),
            pl.BlockSpec(memory_space=pltpu.VMEM),
            pl.BlockSpec(memory_space=pl.ANY),
            pl.BlockSpec(memory_space=pl.ANY),
            pl.BlockSpec(memory_space=pl.ANY),
        ],
        out_specs=pl.BlockSpec(memory_space=pltpu.VMEM),
        scratch_shapes=[
            pltpu.VMEM((32 * tokens, width), jnp.bfloat16),
            pltpu.VMEM((width, packed), jnp.bfloat16),
            pltpu.VMEM((8 * tokens, packed), jnp.float32),
            pltpu.SemaphoreType.DMA((COPIES,)),
            pltpu.SemaphoreType.DMA((COPIES,)),
            pltpu.SemaphoreType.DMA((2,)),
        ],
        compiler_params=pltpu.CompilerParams(collective_id=0, has_side_effects=True),
        name="gather_project",
    )(rows, gain, query_weight, key_weight, value_weight)


def attend_kernel(packing_ref, segment_ref, qkv_ref, out_ref, packed):
    slots = qkv_ref.shape[0]
    heads = out_ref.shape[1] // HDIM
    core = lax.axis_index("dev") % 2
    block = 128
    chunk = 256
    order = jnp.transpose(jnp.broadcast_to(packing_ref[...], (block, slots)))
    segment = jnp.transpose(jnp.broadcast_to(segment_ref[...], (block, slots)))
    for start in range(0, slots, chunk):
        lane = lax.broadcasted_iota(jnp.int32, (chunk, block), 1)
        picked = order[start : start + chunk]
        onehot = jnp.concatenate(
            [
                jnp.where(picked == lane + at, 1.0, 0.0).astype(jnp.bfloat16)
                for at in range(0, slots, block)
            ],
            axis=1,
        )
        packed[pl.ds(start, chunk), :] = jnp.dot(
            onehot, qkv_ref[...], preferred_element_type=jnp.float32
        ).astype(jnp.bfloat16)
    first = packed[:, pl.ds(heads * HDIM, HDIM)]
    second = packed[:, pl.ds((heads + 1) * HDIM, HDIM)]
    keys = jnp.where(core == 0, first, second)
    values = jnp.where(core == 0, second, first)
    for start in range(0, slots, block):
        begin = max(0, start - 2 * block)
        span = start + block - begin
        query = jnp.concatenate(
            [packed[pl.ds(start, block), pl.ds(h * HDIM, HDIM)] for h in range(heads)], axis=0
        )
        scores = lax.dot_general(
            query,
            keys[begin : begin + span],
            (((1,), (1,)), ((), ())),
            preferred_element_type=jnp.float32,
        ) / math.sqrt(HDIM)
        own = jnp.concatenate([segment[start : start + block]] * (span // block), axis=1)
        other = segment_ref[:, pl.ds(begin, span)]
        slot = start + lax.broadcasted_iota(jnp.int32, (block, span), 0)
        key_slot = begin + lax.broadcasted_iota(jnp.int32, (block, span), 1)
        allowed = (own == other) & (key_slot <= slot)
        allowed = jnp.concatenate([allowed.astype(jnp.float32)] * heads, axis=0)
        powers = jnp.where(allowed > 0.5, jnp.exp(scores), 0.0)
        attend = (powers / jnp.sum(powers, axis=1, keepdims=True)).astype(jnp.bfloat16)
        mixed = jnp.dot(attend, values[begin : begin + span], preferred_element_type=jnp.float32)
        for h in range(heads):
            out_ref[pl.ds(start, block), pl.ds(h * HDIM, HDIM)] = mixed[
                h * block : (h + 1) * block
            ].astype(jnp.bfloat16)


def per_device(
    hidden_rows, norm_gain, query_weight, key_weight, value_weight, packing, segment_ids
):
    qkv = project_rows(hidden_rows, norm_gain[None, :], query_weight, key_weight, value_weight)
    slots, wide = qkv.shape[0], query_weight.shape[1]
    return pl.pallas_call(
        attend_kernel,
        out_shape=jax.ShapeDtypeStruct((slots, wide), jnp.bfloat16),
        in_specs=[pl.BlockSpec(memory_space=pltpu.VMEM)] * 3,
        out_specs=pl.BlockSpec(memory_space=pltpu.VMEM),
        scratch_shapes=[pltpu.VMEM(qkv.shape, jnp.bfloat16)],
        name="attend",
    )(packing, segment_ids, qkv)


def solution(mesh):
    in_specs = (
        P(("group", "dev"), None),
        P(),
        P("group", "dev"),
        P("group", None),
        P("group", None),
        P("group", None),
        P("group", None),
    )
    out_specs = P("group", "dev")
    return jax.shard_map(
        per_device, mesh=mesh, in_specs=in_specs, out_specs=out_specs, check_vma=False
    )
```

time: 307 us -> 110 us (0.36)
  waiting for transfers between devices: 231 us -> 0 us
  Pallas kernels: 0 us -> 110 us
  matrix products: 39.6 us -> 0 us
  local copies, waits for them, and re-layouts: 16.7 us -> 0 us
  between operations: 13.2 us -> 0.01 us
  other arithmetic: 6.41 us -> 0 us
    all_gather x4 -> x0, waiting for transfers between devices: 230 us -> none  [the longest x1 112 us: per_device(): gathered = lax.all_gather(source, 'dev', axis=0, tiled=True)]
    pallas_call x0 -> x2, Pallas kernels: none -> 110 us  [the longest x1 104 us: project_rows(): pl.pallas_call(project_kernel, out_shape=jax.ShapeDtypeStruct((32 * token...]
    dot_general x5 -> x0, matrix products: 39.6 us -> none  [the longest x3 33.1 us: add_rows(): return jnp.dot(gathered, weight_rows, preferred_element_type=jnp.float32)]
    gather x3 -> x0, local copies, waits for them, and re-layouts: 11.6 us -> none  [the longest x1 4.31 us: per_device(): key_rows = key_rows[order]]
  transfers between devices with their start and end apart: 4 -> 0, of which waited for: 4 -> 0; matrix products, arithmetic and copies ran while one was open for 12% -> 0% of each run, Pallas kernels for 0% -> 0%
where the time goes in v1:
time: 110 us
  Pallas kernels  110 us (100%)
    pallas_call x1, Pallas kernels, project_rows(): pl.pallas_call(project_kernel, out_shape=jax.ShapeDtypeStruct((32 * token...  104 us
    pallas_call x1, Pallas kernels, per_device(): pl.pallas_call(attend_kernel, out_shape=jax.ShapeDtypeStruct((slots, wide...  5.69 us

profile of v1, /device:TPU:1, one launch (start us, length us, event | category | flops | bytes accessed | tf_op | source)
XLA Modules:
  0.0 110.2 jit_solution(14705495436947792694)
XLA Ops:
  0.0 104.5 %gather_project.1.qkv_ref = bf16[1024,512]{1,0:T(8,128)(2,1)} custom-call(bf16[32,8192]{1,0:T(8,128)(2,1)} %x_ref.1, f32[1,8192]{1,0:T(1,128)} %bitcast.1, bf16[1024,256]{1,0:T(8,128)(2,1)} %wq_ref.1, bf16[1024,1024]{1,0:T(8,128)(2,1)} %wk_ref.1, bf16[1024,1024]{1,0:T(8,128)(2,1)} %wv_ref.1), custom_call_target="tpu_custom_call" | custom-call | tf_op jit(solution)/shard_map/gather_project/pallas_call | solution.py:289
  104.5 5.7 %attend.1 = bf16[1024,256]{1,0:T(8,128)(2,1)} custom-call(s32[1,1024]{1,0:T(1,128)} %packing_ref.1, s32[1,1024]{1,0:T(1,128)} %segment_ref.1, bf16[1024,512]{1,0:T(8,128)(2,1)} %gather_project.1.qkv_ref), custom_call_target="tpu_custom_call" | custom-call | tf_op jit(solution)/shard_map/attend/pallas_call | solution.py:370

commit v2 on v1

--- a/solution.py
+++ b/solution.py
@@ -186,54 +186,54 @@
     send(("d", 1), xslot(0, 0, 0, 1), xslot(2, 0, 0, 1), down)
     send(("n", 0, 0), wslot(0, 0, 0), wslot(0, 0, 0), north)
     send(("t", 0, 1), wslot(0, 0, 1), wslot(0, 0, 1), south)
-    send(("a", 0), wslot(0, 0, 0), wslot(0, 0, 0), across)
     send(("r", 0, 1), xslot(0, 0, 0, 1), xslot(0, 1, 0, 1), right)
     send(("l", 0, 0), xslot(0, 0, 0, 0), xslot(0, 2, 0, 0), left)
     send(("u", 1), xslot(0, 0, 0, 1), xslot(1, 0, 0, 1), up)
     send(("d", 0), xslot(0, 0, 0, 0), xslot(2, 0, 0, 0), down)
     send(("n", 0, 1), wslot(0, 0, 1), wslot(0, 0, 1), north)
     send(("t", 0, 0), wslot(0, 0, 0), wslot(0, 0, 0), south)
-    send(("a", 1), wslot(0, 0, 1), wslot(0, 0, 1), across)
     for h in (0, 1):
         share_x(0, 0, h)
         share_kv(0, 0, h)
 
+    send(("a", 0), wslot(0, 0, 0), wslot(0, 0, 0), across)
+    send(("a", 1), wslot(0, 0, 1), wslot(0, 0, 1), across)
     from_left(0, 0)
     from_right(0, 1)
     from_south(0, 0)
     from_north(0, 1)
+    from_below(0)
+    from_above(1)
     from_left(0, 1)
     from_right(0, 0)
-    from_below(0)
-    from_above(1)
     from_south(0, 1)
     from_north(0, 0)
     from_opposite(0)
-    from_across(0)
+    from_left(1, 0)
+    from_right(2, 1)
     from_below(1)
     from_above(0)
-    from_left(1, 0)
-    from_right(2, 1)
-    from_across(1)
-    from_far(0)
     from_right(1, 0)
     from_left(2, 1)
+    from_far(0)
+    from_across(0)
+    from_across(1)
+    from_left(1, 1)
+    from_right(2, 0)
+    from_right(1, 1)
+    from_left(2, 0)
     arrive(("uo",), xslot(3, 0, 0, 0))
     spread_x(3, 0)
     share_x(3, 0, 0)
     arrive(("do",), xslot(3, 0, 0, 1))
     spread_x(3, 1)
     share_x(3, 0, 1)
-    from_right(1, 1)
-    from_left(2, 0)
     from_south(1, 0)
     from_north(1, 1)
-    from_left(1, 1)
-    from_right(2, 0)
+    from_opposite(1)
+    from_opposite(2)
     from_south(1, 1)
     from_north(1, 0)
-    from_opposite(1)
-    from_opposite(2)
     from_far(1)
 
     def shared_x(zr):

time: 110 us -> 102 us (0.927)
  Pallas kernels: 110 us -> 102 us
    pallas_call x1, Pallas kernels: 104 us -> 95.9 us  [project_rows(): pl.pallas_call(project_kernel, out_shape=jax.ShapeDtypeStruct((32 * token...]
where the time goes in v2:
time: 102 us
  Pallas kernels  102 us (100%)
    pallas_call x1, Pallas kernels, project_rows(): pl.pallas_call(project_kernel, out_shape=jax.ShapeDtypeStruct((32 * token...  95.9 us
    pallas_call x1, Pallas kernels, per_device(): pl.pallas_call(attend_kernel, out_shape=jax.ShapeDtypeStruct((slots, wide...  5.69 us

profile of v2, /device:TPU:1, one launch (start us, length us, event | category | flops | bytes accessed | tf_op | source)
XLA Modules:
  0.0 101.6 jit_solution(8069160937080629009)
XLA Ops:
  0.0 95.9 %gather_project.1.qkv_ref = bf16[1024,512]{1,0:T(8,128)(2,1)} custom-call(bf16[32,8192]{1,0:T(8,128)(2,1)} %x_ref.1, f32[1,8192]{1,0:T(1,128)} %bitcast.1, bf16[1024,256]{1,0:T(8,128)(2,1)} %wq_ref.1, bf16[1024,1024]{1,0:T(8,128)(2,1)} %wk_ref.1, bf16[1024,1024]{1,0:T(8,128)(2,1)} %wv_ref.1), custom_call_target="tpu_custom_call" | custom-call | tf_op jit(solution)/shard_map/gather_project/pallas_call | solution.py:289
  95.9 5.7 %attend.1 = bf16[1024,256]{1,0:T(8,128)(2,1)} custom-call(s32[1,1024]{1,0:T(1,128)} %packing_ref.1, s32[1,1024]{1,0:T(1,128)} %segment_ref.1, bf16[1024,512]{1,0:T(8,128)(2,1)} %gather_project.1.qkv_ref), custom_call_target="tpu_custom_call" | custom-call | tf_op jit(solution)/shard_map/attend/pallas_call | solution.py:370

commit v3 on v2

--- a/solution.py
+++ b/solution.py
@@ -92,21 +92,29 @@
 
     def from_left(zr, h):
         arrive(("r", zr, h), xslot(zr, 1, 0, h))
-        if h == 0:
+        if h == 0 and zr != 3:
             send(("ro", zr), xslot(zr, 1, 0, 0), xslot(zr, 3, 0, 0), right)
         share_x(zr, 1, h)
 
     def from_right(zr, h):
         arrive(("l", zr, h), xslot(zr, 2, 0, h))
-        if h == 1:
+        if h == 1 and zr != 3:
             send(("lo", zr), xslot(zr, 2, 0, 1), xslot(zr, 3, 0, 1), left)
         share_x(zr, 2, h)
 
-    def from_opposite(zr):
-        arrive(("ro", zr), xslot(zr, 3, 0, 0))
-        share_x(zr, 3, 0)
-        arrive(("lo", zr), xslot(zr, 3, 0, 1))
-        share_x(zr, 3, 1)
+    def from_opposite(zr, h):
+        arrive((("ro", "lo")[h], zr), xslot(zr, 3, 0, h))
+        if (zr, h) == (1, 0):
+            send(("uc",), xslot(1, 3, 0, 0), xslot(3, 3, 0, 0), up)
+        if (zr, h) == (2, 1):
+            send(("dc",), xslot(2, 3, 0, 1), xslot(3, 3, 0, 1), down)
+        share_x(zr, 3, h)
+
+    def from_corner():
+        arrive(("uc",), xslot(3, 3, 0, 0))
+        share_x(3, 3, 0)
+        arrive(("dc",), xslot(3, 3, 0, 1))
+        share_x(3, 3, 1)
 
     def spread_w(zlr, h):
         send(("n", zlr, h), wslot(zlr, 0, h), wslot(zlr, 0, h), north)
@@ -148,6 +156,41 @@
         arrive(("a", h), wslot(1, 0, h))
         spread_w(1, h)
         share_kv(1, 0, h)
+
+    def shared_x(zr):
+        for xr in range(4):
+            for h in (0, 1):
+                arrive(("s", zr, xr, h), xslot(zr, xr, 1, h))
+
+    def shared_kv(zlr):
+        for yr in range(4):
+            for h in (0, 1):
+                arrive(("k", zlr, yr, h), kvslot(zlr, yr, h, 1))
+
+    def project(zr, zlr):
+        count = 8 * rows
+        part = pl.ds(zr * count, count)
+        first = (zl if zlr == 0 else 1 - zl) * 4
+        if zlr == 0:
+            acc[part, :] = jnp.zeros((count, acc.shape[1]), jnp.float32)
+
+        def step(k, carry):
+            at = pl.ds(pl.multiple_of((first + k) * slab, slab), slab)
+            acc[part, :] += jnp.dot(
+                xbuf[part, at], wbuf[at, :], preferred_element_type=jnp.float32
+            )
+            return carry
+
+        lax.fori_loop(0, 4, step, 0)
+        if zlr == 0:
+            return
+        for xr in range(4):
+            for cr in range(2):
+                core = c if cr == 0 else 1 - c
+                to = pl.multiple_of(dev_at(SHIFT[xr], SHIFT[zr], core) * rows, rows)
+                out_ref[pl.ds(to, rows), :] = acc[
+                    pl.ds(zr * count + (xr * 2 + cr) * rows, rows), :
+                ].astype(jnp.bfloat16)
 
     own = pl.multiple_of(slab_at(0, 0), slab)
     own_q = pltpu.make_async_copy(
@@ -208,7 +251,8 @@
     from_right(0, 0)
     from_south(0, 1)
     from_north(0, 0)
-    from_opposite(0)
+    from_opposite(0, 0)
+    from_opposite(0, 1)
     from_left(1, 0)
     from_right(2, 1)
     from_below(1)
@@ -228,56 +272,34 @@
     arrive(("do",), xslot(3, 0, 0, 1))
     spread_x(3, 1)
     share_x(3, 0, 1)
+    from_opposite(1, 0)
+    from_opposite(2, 1)
     from_south(1, 0)
     from_north(1, 1)
-    from_opposite(1)
-    from_opposite(2)
+    from_opposite(1, 1)
+    from_opposite(2, 0)
+    shared_kv(0)
+    shared_x(0)
+    project(0, 0)
     from_south(1, 1)
     from_north(1, 0)
-    from_far(1)
-
-    def shared_x(zr):
-        for xr in range(4):
-            for h in (0, 1):
-                arrive(("s", zr, xr, h), xslot(zr, xr, 1, h))
-
-    def project(zr):
-        count = 8 * rows
-        acc[...] = jnp.zeros_like(acc)
-
-        def step(k, carry):
-            at = pl.ds(pl.multiple_of(k * slab, slab), slab)
-            acc[...] += jnp.dot(
-                xbuf[pl.ds(zr * count, count), at], wbuf[at, :], preferred_element_type=jnp.float32
-            )
-            return carry
-
-        lax.fori_loop(0, 8, step, 0)
-        for xr in range(4):
-            for cr in range(2):
-                core = c if cr == 0 else 1 - c
-                to = pl.multiple_of(dev_at(SHIFT[xr], SHIFT[zr], core) * rows, rows)
-                out_ref[pl.ds(to, rows), :] = acc[pl.ds((xr * 2 + cr) * rows, rows), :].astype(
-                    jnp.bfloat16
-                )
-
-    for zlr in range(2):
-        for yr in range(4):
-            for h in (0, 1):
-                arrive(("k", zlr, yr, h), kvslot(zlr, yr, h, 1))
-    shared_x(0)
-    project(0)
+    shared_x(1)
+    project(1, 0)
     from_left(3, 0)
     from_right(3, 1)
-    shared_x(1)
-    project(1)
+    shared_x(2)
+    project(2, 0)
+    from_far(1)
+    shared_kv(1)
+    project(0, 1)
     from_left(3, 1)
     from_right(3, 0)
-    shared_x(2)
-    project(2)
-    from_opposite(3)
+    project(1, 1)
+    project(2, 1)
+    from_corner()
     shared_x(3)
-    project(3)
+    project(3, 0)
+    project(3, 1)
     for copy in started:
         copy.wait_send()
 
@@ -300,7 +322,7 @@
         scratch_shapes=[
             pltpu.VMEM((32 * tokens, width), jnp.bfloat16),
             pltpu.VMEM((width, packed), jnp.bfloat16),
-            pltpu.VMEM((8 * tokens, packed), jnp.float32),
+            pltpu.VMEM((32 * tokens, packed), jnp.float32),
             pltpu.SemaphoreType.DMA((COPIES,)),
             pltpu.SemaphoreType.DMA((COPIES,)),
             pltpu.SemaphoreType.DMA((2,)),

time: 102 us -> 96.7 us (0.948)
  Pallas kernels: 102 us -> 96.5 us
    pallas_call x1, Pallas kernels: 95.9 us -> 90.8 us  [project_rows(): pl.pallas_call(project_kernel, out_shape=jax.ShapeDtypeStruct((32 * token...]
where the time goes in v3:
time: 96.7 us; the launch traced here: 96.5 us
  Pallas kernels  96.5 us (100%)
    pallas_call x1, Pallas kernels, project_rows(): pl.pallas_call(project_kernel, out_shape=jax.ShapeDtypeStruct((32 * token...  90.8 us
    pallas_call x1, Pallas kernels, per_device(): pl.pallas_call(attend_kernel, out_shape=jax.ShapeDtypeStruct((slots, wide...  5.69 us

profile of v3, /device:TPU:1, one launch (start us, length us, event | category | flops | bytes accessed | tf_op | source)
XLA Modules:
  0.0 96.5 jit_solution(15038382127466669315)
XLA Ops:
  0.0 90.8 %gather_project.1.qkv_ref = bf16[1024,512]{1,0:T(8,128)(2,1)} custom-call(bf16[32,8192]{1,0:T(8,128)(2,1)} %x_ref.1, f32[1,8192]{1,0:T(1,128)} %bitcast.1, bf16[1024,256]{1,0:T(8,128)(2,1)} %wq_ref.1, bf16[1024,1024]{1,0:T(8,128)(2,1)} %wk_ref.1, bf16[1024,1024]{1,0:T(8,128)(2,1)} %wv_ref.1), custom_call_target="tpu_custom_call" | custom-call | tf_op jit(solution)/shard_map/gather_project/pallas_call | solution.py:311
  90.8 5.7 %attend.1 = bf16[1024,256]{1,0:T(8,128)(2,1)} custom-call(s32[1,1024]{1,0:T(1,128)} %packing_ref.1, s32[1,1024]{1,0:T(1,128)} %segment_ref.1, bf16[1024,512]{1,0:T(8,128)(2,1)} %gather_project.1.qkv_ref), custom_call_target="tpu_custom_call" | custom-call | tf_op jit(solution)/shard_map/attend/pallas_call | solution.py:392

commit v4 on v3

--- a/solution.py
+++ b/solution.py
@@ -368,7 +368,7 @@
             keys[begin : begin + span],
             (((1,), (1,)), ((), ())),
             preferred_element_type=jnp.float32,
-        ) / math.sqrt(HDIM)
+        ) * (1.0 / math.sqrt(HDIM))
         own = jnp.concatenate([segment[start : start + block]] * (span // block), axis=1)
         other = segment_ref[:, pl.ds(begin, span)]
         slot = start + lax.broadcasted_iota(jnp.int32, (block, span), 0)
@@ -376,7 +376,10 @@
         allowed = (own == other) & (key_slot <= slot)
         allowed = jnp.concatenate([allowed.astype(jnp.float32)] * heads, axis=0)
         powers = jnp.where(allowed > 0.5, jnp.exp(scores), 0.0)
-        attend = (powers / jnp.sum(powers, axis=1, keepdims=True)).astype(jnp.bfloat16)
+        total = jnp.sum(powers, axis=1, keepdims=True)
+        scale = jnp.where(total > 1e30, 0.0625, 1.0)
+        inverse = 1.0 / (total * scale)
+        attend = (powers * scale * inverse).astype(jnp.bfloat16)
         mixed = jnp.dot(attend, values[begin : begin + span], preferred_element_type=jnp.float32)
         for h in range(heads):
             out_ref[pl.ds(start, block), pl.ds(h * HDIM, HDIM)] = mixed[

time: 96.7 us -> 96.7 us (level)
  no operation moved by 1% of the time
where the time goes in v4:
time: 96.7 us; the launch traced here: 96.5 us
  Pallas kernels  96.5 us (100%)
    pallas_call x1, Pallas kernels, project_rows(): pl.pallas_call(project_kernel, out_shape=jax.ShapeDtypeStruct((32 * token...  90.8 us
    pallas_call x1, Pallas kernels, per_device(): pl.pallas_call(attend_kernel, out_shape=jax.ShapeDtypeStruct((slots, wide...  5.7 us

profile of v4, /device:TPU:1, one launch (start us, length us, event | category | flops | bytes accessed | tf_op | source)
XLA Modules:
  0.0 96.5 jit_solution(4011136183560921582)
XLA Ops:
  0.0 90.8 %gather_project.1.qkv_ref = bf16[1024,512]{1,0:T(8,128)(2,1)} custom-call(bf16[32,8192]{1,0:T(8,128)(2,1)} %x_ref.1, f32[1,8192]{1,0:T(1,128)} %bitcast.1, bf16[1024,256]{1,0:T(8,128)(2,1)} %wq_ref.1, bf16[1024,1024]{1,0:T(8,128)(2,1)} %wk_ref.1, bf16[1024,1024]{1,0:T(8,128)(2,1)} %wv_ref.1), custom_call_target="tpu_custom_call" | custom-call | tf_op jit(solution)/shard_map/gather_project/pallas_call | solution.py:311
  90.8 5.7 %attend.1 = bf16[1024,256]{1,0:T(8,128)(2,1)} custom-call(s32[1,1024]{1,0:T(1,128)} %packing_ref.1, s32[1,1024]{1,0:T(1,128)} %segment_ref.1, bf16[1024,512]{1,0:T(8,128)(2,1)} %gather_project.1.qkv_ref), custom_call_target="tpu_custom_call" | custom-call | tf_op jit(solution)/shard_map/attend/pallas_call | solution.py:395
